TPU v7x, 32 devices: a whole 2x2x4 slice. The times are simulated.
32 devices in a mesh: dp: 2 (over y), ctx: 4 (over z), tp: 4 (over x, core).
Axes of the slice: x: 2, y: 2, z: 4, core: 2. Of those that a mesh axis runs over, the one named last changes fastest.
Arguments:
- layer_input: bfloat16 [2, 4096, 1024], P('dp', 'ctx'), may hold values from -6 to 6
- segments: int32 [2, 4096], P('dp', 'ctx'), may hold values from 0 to 16, as said below
- positions: int32 [2, 4096], P('dp', 'ctx'), may hold values from 0 to 4094, as said below
- w_q: bfloat16 [1024, 1024], P('dp', 'tp'), may hold values from -0.1875 to 0.1875
- w_k: bfloat16 [1024, 1024], P('dp', 'tp'), may hold values from -0.1875 to 0.1875
- w_v: bfloat16 [1024, 1024], P('dp', 'tp'), may hold values from -0.1875 to 0.1875
- w_o: bfloat16 [1024, 1024], P('tp', 'dp'), may hold values from -0.75 to 0.75
- w_in: bfloat16 [1024, 4096], P('dp', 'tp'), may hold values from -0.1875 to 0.1875
- w_out: bfloat16 [4096, 1024], P('tp', 'dp'), may hold values from -0.09375 to 0.09375
- ln1_gain: bfloat16 [1024], P('dp'), may hold values from 0.25 to 1.75
- ln1_bias: bfloat16 [1024], P('dp'), may hold values from -1 to 1
- ln2_gain: bfloat16 [1024], P('dp'), may hold values from 0.25 to 1.75
- ln2_bias: bfloat16 [1024], P('dp'), may hold values from -1 to 1
- cotangent: bfloat16 [2, 4096, 1024], P('dp', 'ctx'), may hold values from -6 to 6
Outputs:
- layer_output: float32 [2, 4096, 1024], P('dp', 'ctx')
- x_grad: float32 [2, 4096, 1024], P('dp', 'ctx')
- w_q_grad: float32 [1024, 1024], P('dp', 'tp')
- w_k_grad: float32 [1024, 1024], P('dp', 'tp')
- w_v_grad: float32 [1024, 1024], P('dp', 'tp')
- w_o_grad: float32 [1024, 1024], P('tp', 'dp')
- w_in_grad: float32 [1024, 4096], P('dp', 'tp')
- w_out_grad: float32 [4096, 1024], P('tp', 'dp')
- ln1_gain_grad: float32 [1024], P('dp')
- ln1_bias_grad: float32 [1024], P('dp')
- ln2_gain_grad: float32 [1024], P('dp')
- ln2_bias_grad: float32 [1024], P('dp')
Inputs may be any that keep to these rules, and one draw needn't show every extreme that they name: `segments`: along a sequence the document number never falls; it is 0 at the first slot and 16 at the last. `positions`: A slot's position is its offset from the first slot of its document.
All inputs are finite; a program needn't handle non-finite values.
Results may differ from a plain program's by a relative error of at most 0.023.
Values may be sent and summed in bfloat16 or wider, within the bound.
No kernel may reach another device: no remote copies, remote signals or barrier semaphores. Data moves between devices by JAX's collectives and lax.ppermute only.
A program may use at most 256 MiB of HBM per device.

v0:
```python
import jax
import jax.numpy as jnp
from jax import lax
from jax.sharding import PartitionSpec as P

D = 1024
H = 16
NEG_BIG = -1e30
SQRT_HALF = 0.7071067811865476
INV_SQRT_TAU = 0.3989422804014327


def rotate_heads(values, positions, head_size, sign):
    half = head_size // 2
    freq = 10000.0 ** (-jnp.arange(half, dtype=jnp.float32) * 2.0 / head_size)
    angles = positions.astype(jnp.float32)[..., None] * freq
    cosine = jnp.cos(angles)[..., None, :]
    sine = sign * jnp.sin(angles)[..., None, :]
    first = values[..., :half]
    second = values[..., half:]
    return jnp.concatenate(
        [first * cosine - second * sine, second * cosine + first * sine], axis=-1
    )


def norm_forward(values, gain, shift):
    centered = values - jnp.mean(values, axis=-1, keepdims=True)
    inverse = lax.rsqrt(jnp.mean(centered * centered, axis=-1, keepdims=True) + 1e-05)
    normed = centered * inverse
    return (normed * gain.astype(jnp.float32) + shift.astype(jnp.float32), normed, inverse)


def norm_backward(incoming, normed, inverse, gain):
    scaled = incoming * gain.astype(jnp.float32)
    inner = (
        scaled
        - jnp.mean(scaled, axis=-1, keepdims=True)
        - normed * jnp.mean(scaled * normed, axis=-1, keepdims=True)
    )
    return (inverse * inner, jnp.sum(incoming * normed, axis=0), jnp.sum(incoming, axis=0))


def body(
    layer_input,
    segments,
    positions,
    w_q,
    w_k,
    w_v,
    w_o,
    w_in,
    w_out,
    ln1_gain,
    ln1_bias,
    ln2_gain,
    ln2_bias,
    cotangent,
):
    seqs, piece_len, width = layer_input.shape
    head_size = D // H
    (
        query_weight,
        key_weight,
        value_weight,
        out_weight,
        in_weight,
        down_weight,
        gain_one,
        shift_one,
        gain_two,
        shift_two,
    ) = (
        lax.all_gather(w_q, "dp", axis=0, tiled=True),
        lax.all_gather(w_k, "dp", axis=0, tiled=True),
        lax.all_gather(w_v, "dp", axis=0, tiled=True),
        lax.all_gather(w_o, "dp", axis=1, tiled=True),
        lax.all_gather(w_in, "dp", axis=0, tiled=True),
        lax.all_gather(w_out, "dp", axis=1, tiled=True),
        lax.all_gather(ln1_gain, "dp", axis=0, tiled=True),
        lax.all_gather(ln1_bias, "dp", axis=0, tiled=True),
        lax.all_gather(ln2_gain, "dp", axis=0, tiled=True),
        lax.all_gather(ln2_bias, "dp", axis=0, tiled=True),
    )
    local_width = query_weight.shape[1]
    heads_here = local_width // head_size
    doc_whole = lax.all_gather(segments, "ctx", axis=1, tiled=True)
    full_len = doc_whole.shape[1]
    row_count = seqs * piece_len
    tokens = layer_input.reshape(row_count, width)
    scale = head_size ** (-0.5)
    doc_low = jnp.min(segments, axis=1)
    doc_high = jnp.max(segments, axis=1)
    share = row_count // lax.axis_size("tp")
    offset = lax.axis_index("tp") * share

    def reduce_heads(partial_sum):
        return lax.psum_scatter(
            partial_sum.astype(jnp.bfloat16), "tp", scatter_dimension=0, tiled=True
        ).astype(jnp.float32)

    def spread_rows(rows_low):
        return lax.all_gather(rows_low, "tp", axis=0, tiled=True)

    def own_rows(whole_rows):
        return lax.dynamic_slice_in_dim(whole_rows, offset, share, 0)

    def project(weight):
        return jnp.dot(tokens, weight, preferred_element_type=jnp.float32).reshape(
            seqs, piece_len, heads_here, head_size
        )

    queries = rotate_heads(project(query_weight), positions, head_size, 1.0).astype(jnp.bfloat16)
    keys = rotate_heads(project(key_weight), positions, head_size, 1.0).astype(jnp.bfloat16)
    values = project(value_weight).astype(jnp.bfloat16)

    def touches():
        meets = (doc_low <= jnp.max(doc_whole, axis=1)) & (jnp.min(doc_whole, axis=1) <= doc_high)
        return (jnp.any(meets), doc_whole)

    def masked_scores(key_piece, doc_keys):
        scores = (
            jnp.einsum("sqhd,skhd->shqk", queries, key_piece, preferred_element_type=jnp.float32)
            * scale
        )
        same = segments[:, None, :, None] == doc_keys[:, None, None, :]
        return jnp.where(same, scores, NEG_BIG)

    start_state = (
        jnp.full((seqs, heads_here, piece_len), NEG_BIG, jnp.float32),
        jnp.zeros((seqs, heads_here, piece_len), jnp.float32),
        jnp.zeros((seqs, piece_len, heads_here, head_size), jnp.float32),
    )
    key_piece = lax.all_gather(keys, "ctx", axis=1, tiled=True)
    value_piece = lax.all_gather(values, "ctx", axis=1, tiled=True)
    needed, doc_keys = touches()

    def forward_update(state):
        run_max, run_total, run_out = state
        scores = masked_scores(key_piece, doc_keys)
        new_max = jnp.maximum(run_max, jnp.max(scores, axis=-1))
        weights_now = jnp.exp(scores - new_max[..., None])
        factor = jnp.exp(run_max - new_max)
        new_total = jnp.sum(weights_now, axis=-1)
        added = jnp.einsum(
            "shqk,skhd->sqhd",
            weights_now.astype(jnp.bfloat16),
            value_piece,
            preferred_element_type=jnp.float32,
        )
        new_out = run_out * jnp.swapaxes(factor, 1, 2)[..., None] + added
        return (new_max, new_total, new_out)

    run_max, run_total, run_out = lax.cond(needed, forward_update, lambda state: state, start_state)
    attended = run_out / jnp.swapaxes(run_total, 1, 2)[..., None]
    log_total = run_max + jnp.log(run_total)
    attended_low = attended.astype(jnp.bfloat16).reshape(row_count, local_width)
    mixed = reduce_heads(jnp.dot(attended_low, out_weight, preferred_element_type=jnp.float32))
    token_rows = own_rows(tokens).astype(jnp.float32)
    hidden_one, normed_one, inverse_one = norm_forward(token_rows + mixed, gain_one, shift_one)
    hidden_low = spread_rows(hidden_one.astype(jnp.bfloat16))
    pre_act = jnp.dot(hidden_low, in_weight, preferred_element_type=jnp.float32)
    activated = jax.nn.gelu(pre_act, approximate=False).astype(jnp.bfloat16)
    branch_two = reduce_heads(jnp.dot(activated, down_weight, preferred_element_type=jnp.float32))
    output, normed_two, inverse_two = norm_forward(hidden_one + branch_two, gain_two, shift_two)
    out_grad = own_rows(cotangent.reshape(row_count, width)).astype(jnp.float32)
    second_grad, gain_two_grad, shift_two_grad = norm_backward(
        out_grad, normed_two, inverse_two, gain_two
    )
    second_low = spread_rows(second_grad.astype(jnp.bfloat16))
    down_grad = jnp.einsum("rf,rd->fd", activated, second_low, preferred_element_type=jnp.float32)
    act_grad = jnp.einsum("rd,fd->rf", second_low, down_weight, preferred_element_type=jnp.float32)
    slope = (
        0.5 * (1.0 + jax.scipy.special.erf(pre_act * SQRT_HALF))
        + pre_act * jnp.exp(-0.5 * pre_act * pre_act) * INV_SQRT_TAU
    )
    pre_grad = (act_grad * slope).astype(jnp.bfloat16)
    in_grad = jnp.einsum("rd,rf->df", hidden_low, pre_grad, preferred_element_type=jnp.float32)
    hidden_grad = second_grad + reduce_heads(
        jnp.einsum("rf,df->rd", pre_grad, in_weight, preferred_element_type=jnp.float32)
    )
    first_grad, gain_one_grad, shift_one_grad = norm_backward(
        hidden_grad, normed_one, inverse_one, gain_one
    )
    first_low = spread_rows(first_grad.astype(jnp.bfloat16))
    out_weight_grad = jnp.einsum(
        "rj,rd->jd", attended_low, first_low, preferred_element_type=jnp.float32
    )
    heads_grad = jnp.einsum("rd,jd->rj", first_low, out_weight, preferred_element_type=jnp.float32)
    heads_grad = heads_grad.astype(jnp.bfloat16).reshape(seqs, piece_len, heads_here, head_size)
    row_dot = jnp.swapaxes(jnp.sum(heads_grad.astype(jnp.float32) * attended, axis=-1), 1, 2)
    back_state = (
        jnp.zeros((seqs, piece_len, heads_here, head_size), jnp.float32),
        jnp.zeros((seqs, full_len, heads_here, head_size), jnp.float32),
        jnp.zeros((seqs, full_len, heads_here, head_size), jnp.float32),
    )
    backward_key_piece = lax.all_gather(keys, "ctx", axis=1, tiled=True)
    backward_value_piece = lax.all_gather(values, "ctx", axis=1, tiled=True)
    needed, backward_doc_keys = touches()

    def backward_update(state):
        scores = masked_scores(backward_key_piece, backward_doc_keys)
        probs = jnp.exp(scores - log_total[..., None])
        value_part = jnp.einsum(
            "shqk,sqhd->skhd",
            probs.astype(jnp.bfloat16),
            heads_grad,
            preferred_element_type=jnp.float32,
        )
        prob_grad = jnp.einsum(
            "sqhd,skhd->shqk", heads_grad, backward_value_piece, preferred_element_type=jnp.float32
        )
        score_grad = (probs * (prob_grad - row_dot[..., None])).astype(jnp.bfloat16)
        query_grad = (
            jnp.einsum(
                "shqk,skhd->sqhd",
                score_grad,
                backward_key_piece,
                preferred_element_type=jnp.float32,
            )
            * scale
        )
        key_part = (
            jnp.einsum("shqk,sqhd->skhd", score_grad, queries, preferred_element_type=jnp.float32)
            * scale
        )
        return (query_grad, key_part, value_part)

    query_grad, key_grad_all, value_grad_all = lax.cond(
        needed, backward_update, lambda state: state, back_state
    )
    key_grad, value_grad = (
        lax.psum_scatter(
            key_grad_all.astype(jnp.bfloat16), "ctx", scatter_dimension=1, tiled=True
        ).astype(jnp.float32),
        lax.psum_scatter(
            value_grad_all.astype(jnp.bfloat16), "ctx", scatter_dimension=1, tiled=True
        ).astype(jnp.float32),
    )
    query_low = (
        rotate_heads(query_grad, positions, head_size, -1.0)
        .astype(jnp.bfloat16)
        .reshape(row_count, local_width)
    )
    key_low = (
        rotate_heads(key_grad, positions, head_size, -1.0)
        .astype(jnp.bfloat16)
        .reshape(row_count, local_width)
    )
    value_low = value_grad.astype(jnp.bfloat16).reshape(row_count, local_width)
    query_weight_grad = jnp.einsum(
        "rd,rj->dj", tokens, query_low, preferred_element_type=jnp.float32
    )
    key_weight_grad = jnp.einsum("rd,rj->dj", tokens, key_low, preferred_element_type=jnp.float32)
    value_weight_grad = jnp.einsum(
        "rd,rj->dj", tokens, value_low, preferred_element_type=jnp.float32
    )
    input_part = jnp.einsum(
        "rj,dj->rd", query_low, query_weight, preferred_element_type=jnp.float32
    )
    input_part = input_part + jnp.einsum(
        "rj,dj->rd", key_low, key_weight, preferred_element_type=jnp.float32
    )
    input_part = input_part + jnp.einsum(
        "rj,dj->rd", value_low, value_weight, preferred_element_type=jnp.float32
    )
    input_grad = first_grad + reduce_heads(input_part)
    norm_terms = jnp.stack([gain_one_grad, shift_one_grad, gain_two_grad, shift_two_grad])[None]
    output, input_grad, norm_terms = (
        lax.all_gather(output.astype(jnp.bfloat16), "tp", axis=0, tiled=True).astype(output.dtype),
        lax.all_gather(input_grad.astype(jnp.bfloat16), "tp", axis=0, tiled=True).astype(
            input_grad.dtype
        ),
        lax.all_gather(norm_terms.astype(jnp.bfloat16), "tp", axis=0, tiled=True).astype(
            norm_terms.dtype
        ),
    )
    norm_terms = jnp.sum(norm_terms, axis=0)
    gain_one_grad, shift_one_grad, gain_two_grad, shift_two_grad = (
        norm_terms[0],
        norm_terms[1],
        norm_terms[2],
        norm_terms[3],
    )
    shares = (
        lax.psum_scatter(
            query_weight_grad.astype(jnp.bfloat16), "dp", scatter_dimension=0, tiled=True
        ).astype(jnp.float32),
        lax.psum_scatter(
            key_weight_grad.astype(jnp.bfloat16), "dp", scatter_dimension=0, tiled=True
        ).astype(jnp.float32),
        lax.psum_scatter(
            value_weight_grad.astype(jnp.bfloat16), "dp", scatter_dimension=0, tiled=True
        ).astype(jnp.float32),
        lax.psum_scatter(
            out_weight_grad.astype(jnp.bfloat16), "dp", scatter_dimension=1, tiled=True
        ).astype(jnp.float32),
        lax.psum_scatter(
            in_grad.astype(jnp.bfloat16), "dp", scatter_dimension=0, tiled=True
        ).astype(jnp.float32),
        lax.psum_scatter(
            down_grad.astype(jnp.bfloat16), "dp", scatter_dimension=1, tiled=True
        ).astype(jnp.float32),
        lax.psum_scatter(
            gain_one_grad.astype(jnp.bfloat16), "dp", scatter_dimension=0, tiled=True
        ).astype(jnp.float32),
        lax.psum_scatter(
            shift_one_grad.astype(jnp.bfloat16), "dp", scatter_dimension=0, tiled=True
        ).astype(jnp.float32),
        lax.psum_scatter(
            gain_two_grad.astype(jnp.bfloat16), "dp", scatter_dimension=0, tiled=True
        ).astype(jnp.float32),
        lax.psum_scatter(
            shift_two_grad.astype(jnp.bfloat16), "dp", scatter_dimension=0, tiled=True
        ).astype(jnp.float32),
    )
    totals = (
        lax.psum(shares[0].astype(jnp.bfloat16), "ctx").astype(jnp.float32),
        lax.psum(shares[1].astype(jnp.bfloat16), "ctx").astype(jnp.float32),
        lax.psum(shares[2].astype(jnp.bfloat16), "ctx").astype(jnp.float32),
        lax.psum(shares[3].astype(jnp.bfloat16), "ctx").astype(jnp.float32),
        lax.psum(shares[4].astype(jnp.bfloat16), "ctx").astype(jnp.float32),
        lax.psum(shares[5].astype(jnp.bfloat16), "ctx").astype(jnp.float32),
        lax.psum(shares[6].astype(jnp.bfloat16), "ctx").astype(jnp.float32),
        lax.psum(shares[7].astype(jnp.bfloat16), "ctx").astype(jnp.float32),
        lax.psum(shares[8].astype(jnp.bfloat16), "ctx").astype(jnp.float32),
        lax.psum(shares[9].astype(jnp.bfloat16), "ctx").astype(jnp.float32),
    )
    return (
        output.reshape(seqs, piece_len, width),
        input_grad.reshape(seqs, piece_len, width),
        totals[0],
        totals[1],
        totals[2],
        totals[3],
        totals[4],
        totals[5],
        totals[6],
        totals[7],
        totals[8],
        totals[9],
    )


def solution(mesh):
    return jax.shard_map(
        body,
        mesh=mesh,
        in_specs=(
            P("dp", "ctx", None),
            P("dp", "ctx"),
            P("dp", "ctx"),
            P("dp", "tp"),
            P("dp", "tp"),
            P("dp", "tp"),
            P("tp", "dp"),
            P("dp", "tp"),
            P("tp", "dp"),
            P("dp"),
            P("dp"),
            P("dp"),
            P("dp"),
            P("dp", "ctx", None),
        ),
        out_specs=(
            P("dp", "ctx", None),
            P("dp", "ctx", None),
            P("dp", "tp"),
            P("dp", "tp"),
            P("dp", "tp"),
            P("tp", "dp"),
            P("dp", "tp"),
            P("tp", "dp"),
            P("dp"),
            P("dp"),
            P("dp"),
            P("dp"),
        ),
        check_vma=False,
    )
```

profile of v0, /device:TPU:0, one launch (start us, length us, event | category | flops | bytes accessed | tf_op | source)
XLA Modules:
  0.0 972.7 jit_solution(8596426434265717203)
XLA Ops:
  8.1 10.4 %all_gather.63 = bf16[1024,256]{1,0:T(8,128)(2,1)S(1)} all-gather(bf16[512,256]{1,0:T(8,128)(2,1)} %param.23), channel_id=1, replica_groups=mesh['dp'=2,'ctx'=4,'tp'=4] {'dp'}, dimensions={0}, use_global_device_ids=true | all-gather | bytes 786432 | tf_op jit(solution)/shard_map/all_gather | solution.py:75
  21.9 8.1 all_gather.61
  30.3 7.3 all_gather.60
  45.1 13.8 %all_gather.59 = s32[1,4096]{1,0:T(1,128)S(1)} all-gather(s32[1,1024]{1,0:T(1,128)S(1)} %copy-done.25), channel_id=1, replica_groups=mesh['dp'=2,'ctx'=4,'tp'=4] {'ctx'}, dimensions={1}, use_global_device_ids=true | all-gather | bytes 20480 | tf_op jit(solution)/shard_map/all_gather | solution.py:86
  62.8 7.0 all_gather.65
  69.8 46.2 %all-gather.15.cloned.1.call-done = bf16[1,4096,4,64]{1,3,2,0:T(8,128)(2,1)} async-done(((bf16[1,1024,4,64]{1,3,2,0:T(8,128)(2,1)}), bf16[1,4096,4,64]{1,3,2,0:T(8,128)(2,1)}) %all-gather.15.cloned.1.call-update) | async-done | bytes 2097168 | tf_op jit(solution)/shard_map/all_gather | solution.py:133
  116.0 81.0 %conditional.2 = (f32[1,4,1024]{2,1,0:T(4,128)S(1)}, f32[1,4,1024]{2,1,0:T(4,128)}, f32[1,1024,4,64]{1,3,2,0:T(8,128)S(1)}, f32[1,4,1024]{2,1,0:T(4,128)S(1)}) conditional(s32[]{:T(128)} %convert_element_type.302, () %tuple.32, (s32[1,1024]{1,0:T(1,128)S(1)}, s32[1,4096]{1,0:T(1,128)S(1)}, bf16[1,1024,4,64]{1,3,2,0:T(8,128)(2,1)S(1)}, ...), branch_computations={%region_4.0_spmd, %region_5.8_spmd} | conditional | flops 4483981312 | bytes 232476736 | solution.py:153
  116.2 4.7 broadcast_compare_fusion
  120.9 25.9 %fusion = (f32[4,1024]{1,0:T(4,128)S(1)}, f32[4,1024,4096]{2,1,0:T(8,128)}) fusion(pred[1024,4096]{1,0:T(8,128)(4,1)} %broadcast_compare_fusion, bf16[1,4096,4,64]{1,3,2,0:T(8,128)(2,1)S(1)} %copy-done.2, bf16[1,1024,4,64]{1,3,2,0:T(8,128)(2,1)S(1)} %get-tuple-element.51), kind=kOutput, calls=%fused_computation.2 | convolution fusion | flops 2197811200 | bytes 73940992 | tf_op jit(solution)/shard_map/cond/branch_1_fun/sqhd,skhd->shqk/dot_general | solution.py:122
  146.8 23.3 %fusion.2 = f32[4,1024]{1,0:T(4,128)} fusion(f32[4,1024,4096]{2,1,0:T(8,128)} %get-tuple-element.155, f32[4,1024]{1,0:T(4,128)S(1)} %broadcast_maximum_fusion, pred[1024,4096]{1,0:T(8,128)(4,1)} %broadcast_compare_fusion), kind=kLoop, calls=%fused_computation.4 | loop fusion | flops 67104768 | bytes 71335936 | tf_op jit(solution)/shard_map/cond/branch_1_fun/reduce_sum | solution.py:143
  170.9 26.1 %fusion.14 = f32[1,1024,4,64]{1,3,2,0:T(8,128)S(1)} fusion(bf16[1,4096,4,64]{1,3,2,0:T(8,128)(2,1)} %get-tuple-element.53, f32[4,1024,4096]{2,1,0:T(8,128)} %get-tuple-element.155, f32[4,1024]{1,0:T(4,128)S(1)} %broadcast_maximum_fusion, pred[1024,4096]{1,0:T(8,128)(4,1)} %broadcast_compare_fusion, f32[1024,4]{0,1:T(4,128)S(1)} %get-tuple-element.144), kind=kOutput, calls=%fused_computation.12 | convolution fusion | flops 2214854656 | bytes 74481664 | tf_op jit(solution)/shard_map/cond/branch_1_fun/shqk,skhd->sqhd/dot_general | solution.py:144
  201.4 4.4 all-gather.1
  205.8 4.4 all-gather.2
  210.2 20.7 %reduce-scatter.13.cloned.1.call-done = bf16[256,1024]{1,0:T(8,128)(2,1)} async-done(((bf16[1024,1024]{1,0:T(8,128)(2,1)}), bf16[256,1024]{1,0:T(8,128)(2,1)}) %reduce-scatter.13.cloned.1.call-update) | async-done | bytes 524304 | tf_op jit(solution)/shard_map/reduce_scatter | solution.py:97
  236.8 22.2 %all-gather.17.cloned.1.call-done = bf16[1024,1024]{1,0:T(8,128)(2,1)} async-done(((bf16[256,1024]{1,0:T(8,128)(2,1)}), bf16[1024,1024]{1,0:T(8,128)(2,1)}) %all-gather.17.cloned.1.call-update) | async-done | bytes 2097168 | tf_op jit(solution)/shard_map/all_gather | solution.py:102
  259.1 14.3 %fusion.50 = (bf16[1024,1024]{1,0:T(8,128)(2,1)}, f32[1024,1024]{1,0:T(8,128)}) fusion(bf16[1024,1024]{1,0:T(8,128)(2,1)} %all-gather.17.cloned.1.call-done, bf16[1024,1024]{1,0:T(8,128)(2,1)} %all-gather.19.cloned.1.call-done), kind=kOutput, calls=%fused_computation.46 | convolution fusion | flops 2215641088 | bytes 10485760 | tf_op jit(solution)/shard_map/dot_general | solution.py:161
  273.4 20.1 %all-gather.21.cloned.1.call-done = bf16[1024,1024]{1,0:T(8,128)(2,1)} async-done(((bf16[1024,512]{1,0:T(8,128)(2,1)}), bf16[1024,1024]{1,0:T(8,128)(2,1)}) %all-gather.21.cloned.1.call-update) | async-done | bytes 2097168 | tf_op jit(solution)/shard_map/all_gather | solution.py:78
  293.5 5.9 convolution_convert_fusion.3
  299.5 4.4 all-gather.3
  303.9 4.4 all-gather.4
  308.3 22.5 %reduce-scatter.15.cloned.1.call-done = bf16[256,1024]{1,0:T(8,128)(2,1)} async-done(((bf16[1024,1024]{1,0:T(8,128)(2,1)}), bf16[256,1024]{1,0:T(8,128)(2,1)}) %reduce-scatter.15.cloned.1.call-update) | async-done | bytes 524304 | tf_op jit(solution)/shard_map/reduce_scatter | solution.py:97
  337.5 22.5 %all-gather.25.cloned.1.call-done = bf16[1024,1024]{1,0:T(8,128)(2,1)} async-done(((bf16[256,1024]{1,0:T(8,128)(2,1)}), bf16[1024,1024]{1,0:T(8,128)(2,1)}) %all-gather.25.cloned.1.call-update) | async-done | bytes 2097168 | tf_op jit(solution)/shard_map/all_gather | solution.py:102
  360.0 6.3 fusion.56
  371.5 31.3 %reduce-scatter.17.cloned.1.call-done = bf16[256,1024]{1,0:T(8,128)(2,1)} async-done(((bf16[1024,1024]{1,0:T(8,128)(2,1)}), bf16[256,1024]{1,0:T(8,128)(2,1)}) %reduce-scatter.17.cloned.1.call-update) | async-done | bytes 524304 | tf_op jit(solution)/shard_map/reduce_scatter | solution.py:97
  408.0 22.7 %all-gather.27.cloned.1.call-done = bf16[1024,1024]{1,0:T(8,128)(2,1)} async-done(((bf16[256,1024]{1,0:T(8,128)(2,1)}), bf16[1024,1024]{1,0:T(8,128)(2,1)}) %all-gather.27.cloned.1.call-update) | async-done | bytes 2097168 | tf_op jit(solution)/shard_map/all_gather | solution.py:102
  434.2 129.8 %conditional.3 = (bf16[1,4096,4,64]{1,3,2,0:T(8,128)(2,1)}, bf16[1,4096,4,64]{1,3,2,0:T(8,128)(2,1)}, f32[1,1024,4,32]{1,3,2,0:T(8,128)}, f32[1,1024,4,32]{1,3,2,0:T(8,128)S(1)}) conditional(s32[]{:T(128)} %convert_element_type.302, () %tuple.34, (s32[1,1024]{1,0:T(1,128)S(1)}, s32[1,4096]{1,0:T(1,128)S(1)}, ...), branch_computations={%region_20.21_spmd, %region_21.22_spmd} | conditional | flops 10911748096 | bytes 349294720 | solution.py:228
  434.3 4.7 broadcast_compare_fusion.1
  439.0 23.1 %fusion.34 = f32[4,1024,4096]{2,1,0:T(8,128)} fusion(bf16[1,4096,4,64]{1,3,2,0:T(8,128)(2,1)S(1)} %get-tuple-element.57, bf16[1,1024,4,64]{1,3,2,0:T(8,128)(2,1)S(1)} %get-tuple-element.56), kind=kOutput, calls=%fused_computation.31 | convolution fusion | flops 2147483648 | bytes 69730304 | tf_op jit(solution)/shard_map/cond/branch_1_fun/sqhd,skhd->shqk/dot_general | solution.py:122
  462.2 28.2 %fusion.28 = bf16[1,4096,4,64]{1,3,2,0:T(8,128)(2,1)} fusion(f32[4,1024,4096]{2,1,0:T(8,128)} %fusion.34, f32[4,1024]{1,0:T(4,128)S(1)} %add_bitcast_fusion, pred[1024,4096]{1,0:T(8,128)(4,1)} %broadcast_compare_fusion.1, bf16[1,1024,4,64]{1,3,2,0:T(8,128)(2,1)S(1)} %get-tuple-element.60), kind=kOutput, calls=%fused_computation.27 | convolution fusion | flops 2214592512 | bytes 73940992 | tf_op jit(solution)/shard_map/cond/branch_1_fun/shqk,sqhd->skhd/dot_general | solution.py:203
  490.3 41.9 %multiply_convert_fusion = bf16[4,1024,4096]{2,1,0:T(8,128)(2,1)} fusion(f32[4,1024,4096]{2,1,0:T(8,128)} %fusion.34, f32[4,1024]{1,0:T(4,128)S(1)} %bitcast.238, f32[4,1024]{1,0:T(4,128)S(1)} %add_bitcast_fusion, pred[1024,4096]{1,0:T(8,128)(4,1)} %broadcast_compare_fusion.1, bf16[1,4096,4,64]{1,3,2,0:T(8,128)(2,1)} %get-tuple-element.61, ...), kind=kOutput, calls=%fused_computation.19 | convolution fusion | flops 2248146944 | bytes 107511808 | tf_op jit(solution)/shard_map/cond/branch_1_fun/sqhd,skhd->shqk/dot_general | solution.py:209
  532.2 15.6 %fusion.39 = f32[1,1024,4,64]{1,3,2,0:T(8,128)S(1)} fusion(bf16[4,1024,4096]{2,1,0:T(8,128)(2,1)} %multiply_convert_fusion, bf16[1,4096,4,64]{1,3,2,0:T(8,128)(2,1)S(1)} %copy-done.4), kind=kOutput, calls=%fused_computation.34 | convolution fusion | flops 2147745792 | bytes 36700160 | tf_op jit(solution)/shard_map/cond/branch_1_fun/shqk,skhd->sqhd/dot_general | solution.py:214
  547.8 15.1 %fusion.27 = bf16[1,4096,4,64]{1,3,2,0:T(8,128)(2,1)} fusion(bf16[4,1024,4096]{2,1,0:T(8,128)(2,1)} %multiply_convert_fusion, bf16[1,1024,4,64]{1,3,2,0:T(8,128)(2,1)S(1)} %get-tuple-element.56), kind=kOutput, calls=%fused_computation.26 | convolution fusion | flops 2149580800 | bytes 36175872 | tf_op jit(solution)/shard_map/cond/branch_1_fun/shqk,sqhd->skhd/dot_general | solution.py:223
  565.6 5.3 convolution_convert_fusion.1
  571.0 6.0 convolution_convert_fusion
  580.4 27.4 %reduce-scatter.21.cloned.1.call-done = bf16[1,1024,4,64]{1,3,2,0:T(8,128)(2,1)} async-done(((bf16[1,4096,4,64]{1,3,2,0:T(8,128)(2,1)}), bf16[1,1024,4,64]{1,3,2,0:T(8,128)(2,1)}) %reduce-scatter.21.cloned.1.call-update) | async-done | bytes 524304 | tf_op jit(solution)/shard_map/reduce_scatter | solution.py:235
  610.4 43.1 %reduce-scatter.19.cloned.1.call-done = bf16[1,1024,4,64]{1,3,2,0:T(8,128)(2,1)} async-done(((bf16[1,4096,4,64]{1,3,2,0:T(8,128)(2,1)}), bf16[1,1024,4,64]{1,3,2,0:T(8,128)(2,1)}) %reduce-scatter.19.cloned.1.call-update) | async-done | bytes 524304 | tf_op jit(solution)/shard_map/reduce_scatter | solution.py:232
  667.2 20.3 %reduce-scatter.33.cloned.1.call-done = bf16[512,1024]{1,0:T(8,128)(2,1)} async-done(((bf16[1024,1024]{1,0:T(8,128)(2,1)}), bf16[512,1024]{1,0:T(8,128)(2,1)}) %reduce-scatter.33.cloned.1.call-update) | async-done | bytes 1048592 | tf_op jit(solution)/shard_map/reduce_scatter | solution.py:297
  687.5 34.2 %reduce-scatter.35.cloned.1.call-done = bf16[1024,512]{1,0:T(8,128)(2,1)} async-done(((bf16[1024,1024]{1,0:T(8,128)(2,1)}), bf16[1024,512]{1,0:T(8,128)(2,1)}) %reduce-scatter.35.cloned.1.call-update) | async-done | bytes 1048592 | tf_op jit(solution)/shard_map/reduce_scatter | solution.py:300
  721.7 16.8 %reduce-scatter.31.cloned.1.call-done = bf16[256,512]{1,0:T(8,128)(2,1)} async-done(((bf16[256,1024]{1,0:T(8,128)(2,1)}), bf16[256,512]{1,0:T(8,128)(2,1)}) %reduce-scatter.31.cloned.1.call-update) | async-done | bytes 262160 | tf_op jit(solution)/shard_map/reduce_scatter | solution.py:294
  738.5 17.5 %reduce-scatter.29.cloned.1.call-done = bf16[512,256]{0,1:T(8,128)(2,1)} async-done(((bf16[1024,256]{0,1:T(8,128)(2,1)}), bf16[512,256]{0,1:T(8,128)(2,1)}) %reduce-scatter.29.cloned.1.call-update) | async-done | bytes 262160 | tf_op jit(solution)/shard_map/reduce_scatter | solution.py:291
  756.0 17.3 %reduce-scatter.27.cloned.1.call-done = bf16[512,256]{0,1:T(8,128)(2,1)} async-done(((bf16[1024,256]{0,1:T(8,128)(2,1)}), bf16[512,256]{0,1:T(8,128)(2,1)}) %reduce-scatter.27.cloned.1.call-update) | async-done | bytes 262160 | tf_op jit(solution)/shard_map/reduce_scatter | solution.py:288
  773.3 17.5 %reduce-scatter.25.cloned.1.call-done = bf16[512,256]{0,1:T(8,128)(2,1)} async-done(((bf16[1024,256]{0,1:T(8,128)(2,1)}), bf16[512,256]{0,1:T(8,128)(2,1)}) %reduce-scatter.25.cloned.1.call-update) | async-done | bytes 262160 | tf_op jit(solution)/shard_map/reduce_scatter | solution.py:285
  790.9 34.1 %reduce-scatter.23.cloned.1.call-done = bf16[256,1024]{1,0:T(8,128)(2,1)} async-done(((bf16[1024,1024]{1,0:T(8,128)(2,1)}), bf16[256,1024]{1,0:T(8,128)(2,1)}) %reduce-scatter.23.cloned.1.call-update) | async-done | bytes 524304 | tf_op jit(solution)/shard_map/reduce_scatter | solution.py:97
  829.5 4.4 bitcast_convert_fusion.1
  833.9 5.3 all_gather.77
  839.3 5.0 all-reduce.6
  844.6 12.0 %all-reduce.4 = (bf16[512]{0:T(512)(128)(2,1)S(1)}, bf16[512]{0:T(512)(128)(2,1)S(1)}, bf16[512]{0:T(512)(128)(2,1)S(1)}, bf16[512]{0:T(512)(128)(2,1)S(1)}) all-reduce(bf16[512]{0:T(512)(128)(2,1)S(1)} %dynamic-slice.3, bf16[512]{0:T(512)(128)(2,1)S(1)} %dynamic-slice.5, ...), channel_id=1, replica_groups=mesh['dp'=2,'ctx'=4,'tp'=4] {'ctx'}, use_global_device_ids=true, to_apply=%region_43.44 | all-reduce | flops 2048 | bytes 8192 | tf_op jit(solution)/shard_map/psum | solution.py:323
  859.0 90.2 %all-reduce.9.cloned.1.call-done = (bf16[512,256]{0,1:T(8,128)(2,1)}, bf16[512,256]{0,1:T(8,128)(2,1)}, bf16[512,256]{0,1:T(8,128)(2,1)}, bf16[256,512]{1,0:T(8,...) async-done(((bf16[512,256]{0,1:T(8,128)(2,1)}, bf16[512,256]{0,1:T(8,128)(2,1)}, bf16[512,256]{0,1:T(8,128)(2,1)}, bf16[256,512]{1,0:T(8,128)(2,1)}, ...) | async-done | bytes 3145744 | tf_op jit(solution)/shard_map/psum | solution.py:317
  (208 shorter events, 88.6 us)
Async XLA Ops:
  8.0 13.9 %copy-start.29 = (s32[1,1024]{1,0:T(1,128)S(1)}, s32[1,1024]{1,0:T(1,128)}, u32[]{:S(2)}) copy-start(s32[1,1024]{1,0:T(1,128)} %param.20) | copy-start | bytes 12292
  8.0 13.9 %copy-start.22 = (bf16[512,256]{1,0:T(8,128)(2,1)S(1)}, bf16[512,256]{1,0:T(8,128)(2,1)}, u32[]{:S(2)}) copy-start(bf16[512,256]{1,0:T(8,128)(2,1)} %param.22) | copy-start | bytes 786436
  8.0 61.8 %all-gather.31.cloned.1.call-start = ((), (), s32[]{:S(2)}) async-start(), calls=%async_computation.32 | async-start | bytes 2621440 | tf_op jit(solution)/shard_map/all_gather | solution.py:134
  18.4 11.9 %copy-start.5 = (bf16[1024,256]{1,0:T(8,128)(2,1)}, bf16[1024,256]{1,0:T(8,128)(2,1)S(1)}, u32[]{:S(2)}) copy-start(bf16[1024,256]{1,0:T(8,128)(2,1)S(1)} %all_gather.63) | copy-start | bytes 1572868
  18.4 11.9 %copy-start.23 = (bf16[512,256]{1,0:T(8,128)(2,1)S(1)}, bf16[512,256]{1,0:T(8,128)(2,1)}, u32[]{:S(2)}) copy-start(bf16[512,256]{1,0:T(8,128)(2,1)} %param.21) | copy-start | bytes 786436
  21.9 94.1 %all-gather.15.cloned.1.call-start = ((), (), s32[]{:S(2)}) async-start(), calls=%async_computation.12 | async-start | bytes 2621440 | tf_op jit(solution)/shard_map/all_gather | solution.py:133
  30.1 13.7 %copy-start.7 = (bf16[1024,256]{1,0:T(8,128)(2,1)}, bf16[1024,256]{1,0:T(8,128)(2,1)S(1)}, u32[]{:S(2)}) copy-start(bf16[1024,256]{1,0:T(8,128)(2,1)S(1)} %all_gather.61) | copy-start | bytes 1572868
  37.6 6.2 copy-start.9
  43.8 19.0 %copy-start.24 = (bf16[256,512]{1,0:T(8,128)(2,1)S(1)}, bf16[256,512]{1,0:T(8,128)(2,1)}, u32[]{:S(2)}) copy-start(bf16[256,512]{1,0:T(8,128)(2,1)} %param.24) | copy-start | bytes 786436
  45.0 185.9 %reduce-scatter.13.cloned.1.call-start = ((), (), s32[]{:S(2)}) async-start(), calls=%async_computation.13 | async-start | bytes 2621440 | tf_op jit(solution)/shard_map/reduce_scatter | solution.py:97
  69.8 128.1 %copy-start.15 = (bf16[256,1024]{1,0:T(8,128)(2,1)}, bf16[256,1024]{1,0:T(8,128)(2,1)S(1)}, u32[]{:S(2)}) copy-start(bf16[256,1024]{1,0:T(8,128)(2,1)S(1)} %all_gather.65) | copy-start | bytes 1572868
  197.0 8.8 copy-start.31
  200.8 36.0 %all-gather.19.cloned.1.call-start = ((), (), s32[]{:S(2)}) async-start(), calls=%async_computation.15 | async-start | bytes 3145728 | tf_op jit(solution)/shard_map/all_gather | solution.py:77
  201.4 57.7 %all-gather.17.cloned.1.call-start = ((), (), s32[]{:S(2)}) async-start(), calls=%async_computation.14 | async-start | bytes 2621440 | tf_op jit(solution)/shard_map/all_gather | solution.py:102
  236.1 57.3 %all-gather.21.cloned.1.call-start = ((), (), s32[]{:S(2)}) async-start(), calls=%async_computation.16 | async-start | bytes 3145728 | tf_op jit(solution)/shard_map/all_gather | solution.py:78
  236.7 94.0 %reduce-scatter.15.cloned.1.call-start = ((), (), s32[]{:S(2)}) async-start(), calls=%async_computation.17 | async-start | bytes 2621440 | tf_op jit(solution)/shard_map/reduce_scatter | solution.py:97
  293.5 6.0 copy-start.32
  293.5 10.4 %copy-start.33 = (bf16[512]{0:T(512)(128)(2,1)S(1)}, bf16[512]{0:T(512)(128)(2,1)}, u32[]{:S(2)}) copy-start(bf16[512]{0:T(512)(128)(2,1)} %param.30) | copy-start | bytes 3076
  293.5 37.3 %copy-start = (bf16[256,1024]{1,0:T(8,128)(2,1)S(1)}, bf16[256,1024]{1,0:T(8,128)(2,1)}, u32[]{:S(2)}) copy-start(bf16[256,1024]{1,0:T(8,128)(2,1)} %reduce-scatter.13.cloned.1.call-done) | copy-start | bytes 1572868
  299.4 60.6 %all-gather.25.cloned.1.call-start = ((), (), s32[]{:S(2)}) async-start(), calls=%async_computation.19 | async-start | bytes 2621440 | tf_op jit(solution)/shard_map/all_gather | solution.py:102
  337.3 65.5 %reduce-scatter.17.cloned.1.call-start = ((), (), s32[]{:S(2)}) async-start(), calls=%async_computation.20 | async-start | bytes 2621440 | tf_op jit(solution)/shard_map/reduce_scatter | solution.py:97
  360.0 7.7 copy-start.35
  371.5 59.3 %all-gather.27.cloned.1.call-start = ((), (), s32[]{:S(2)}) async-start(), calls=%async_computation.21 | async-start | bytes 2621440 | tf_op jit(solution)/shard_map/all_gather | solution.py:102
  408.0 199.8 %reduce-scatter.21.cloned.1.call-start = ((), (), s32[]{:S(2)}) async-start(), calls=%async_computation.23 | async-start | bytes 2621440 | tf_op jit(solution)/shard_map/reduce_scatter | solution.py:235
  434.3 27.9 %copy-start.20 = (bf16[1,1024,4,64]{1,3,2,0:T(8,128)(2,1)}, bf16[1,1024,4,64]{1,3,2,0:T(8,128)(2,1)S(1)}, u32[]{:S(2)}) copy-start(bf16[1,1024,4,64]{1,3,2,0:T(8,128)(2,1)S(1)} %get-tuple-element.60) | copy-start | bytes 1572868 | tf_op jit(solution)/shard_map/cond
  490.3 41.9 %copy-start.4 = (bf16[1,4096,4,64]{1,3,2,0:T(8,128)(2,1)S(1)}, bf16[1,4096,4,64]{1,3,2,0:T(8,128)(2,1)}, u32[]{:S(2)}) copy-start(bf16[1,4096,4,64]{1,3,2,0:T(8,128)(2,1)} %copy-done.3) | copy-start | bytes 6291460 | tf_op jit(solution)/shard_map/cond
  564.0 89.5 %reduce-scatter.19.cloned.1.call-start = ((), (), s32[]{:S(2)}) async-start(), calls=%async_computation.22 | async-start | bytes 2621440 | tf_op jit(solution)/shard_map/reduce_scatter | solution.py:232
  564.8 122.7 %reduce-scatter.33.cloned.1.call-start = ((), (), s32[]{:S(2)}) async-start(), calls=%async_computation.30 | async-start | bytes 3145728 | tf_op jit(solution)/shard_map/reduce_scatter | solution.py:297
  570.9 6.1 copy-start.14
  570.9 150.8 %reduce-scatter.35.cloned.1.call-start = ((), (), s32[]{:S(2)}) async-start(), calls=%async_computation.31 | async-start | bytes 3145728 | tf_op jit(solution)/shard_map/reduce_scatter | solution.py:300
  577.0 30.9 %copy-start.11 = (bf16[1,1024,1024]{2,1,0:T(8,128)(2,1)S(1)}, bf16[1,1024,1024]{2,1,0:T(8,128)(2,1)}, u32[]{:S(2)}) copy-start(bf16[1,1024,1024]{2,1,0:T(8,128)(2,1)} %param.18) | copy-start | bytes 6291460
  577.0 77.7 %copy-start.17 = (f32[1024,32]{0,1:T(8,128)S(1)}, f32[1024,32]{0,1:T(8,128)}, u32[]{:S(2)}) copy-start(f32[1024,32]{0,1:T(8,128)} %copy-done.16) | copy-start | bytes 393220
  577.0 77.7 %copy-start.21 = (f32[1024,32]{0,1:T(8,128)S(1)}, f32[1024,32]{0,1:T(8,128)}, u32[]{:S(2)}) copy-start(f32[1024,32]{0,1:T(8,128)} %get-tuple-element.169) | copy-start | bytes 393220
  577.0 161.5 %reduce-scatter.31.cloned.1.call-start = ((), (), s32[]{:S(2)}) async-start(), calls=%async_computation.29 | async-start | bytes 786432 | tf_op jit(solution)/shard_map/reduce_scatter | solution.py:294
  580.3 175.6 %reduce-scatter.29.cloned.1.call-start = ((), (), s32[]{:S(2)}) async-start(), calls=%async_computation.28 | async-start | bytes 786432 | tf_op jit(solution)/shard_map/reduce_scatter | solution.py:291
  610.4 162.9 %reduce-scatter.27.cloned.1.call-start = ((), (), s32[]{:S(2)}) async-start(), calls=%async_computation.27 | async-start | bytes 786432 | tf_op jit(solution)/shard_map/reduce_scatter | solution.py:288
  656.2 6.5 copy-start.10
  659.3 131.5 %reduce-scatter.25.cloned.1.call-start = ((), (), s32[]{:S(2)}) async-start(), calls=%async_computation.26 | async-start | bytes 786432 | tf_op jit(solution)/shard_map/reduce_scatter | solution.py:285
  662.6 162.3 %reduce-scatter.23.cloned.1.call-start = ((), (), s32[]{:S(2)}) async-start(), calls=%async_computation.24 | async-start | bytes 2621440 | tf_op jit(solution)/shard_map/reduce_scatter | solution.py:97
  666.4 158.6 %copy-start.12 = (f32[256,1024]{1,0:T(8,128)S(1)}, f32[256,1024]{1,0:T(8,128)}, u32[]{:S(2)}) copy-start(f32[256,1024]{1,0:T(8,128)} %get-tuple-element.147) | copy-start | bytes 3145732
  666.4 161.8 %copy-start.36 = (u32[32]{0:T(128)S(1)}, u32[32]{0:T(128)}, u32[]{:S(2)}) copy-start(u32[32]{0:T(128)} %constant.140) | copy-start | bytes 388
  666.4 163.0 %copy-start.26 = (bf16[1024]{0:T(1024)(128)(2,1)S(1)}, bf16[1024]{0:T(1024)(128)(2,1)}, u32[]{:S(2)}) copy-start(bf16[1024]{0:T(1024)(128)(2,1)} %get-tuple-element.117) | copy-start | bytes 6148
  666.4 163.1 %all-gather.23.cloned.1.call-start = ((), (), s32[]{:S(2)}) async-start(), calls=%async_computation.18 | async-start | bytes 2621440 | tf_op jit(solution)/shard_map/all_gather | solution.py:269
  667.1 282.0 %all-reduce.9.cloned.1.call-start = ((), (), s32[]{:S(2)}) async-start(), calls=%async_computation.33 | async-start | bytes 6291456 | tf_op jit(solution)/shard_map/psum | solution.py:317
  790.8 170.3 %all-gather.29.cloned.1.call-start = ((), (), s32[]{:S(2)}) async-start(), calls=%async_computation.25 | async-start | bytes 2621440 | tf_op jit(solution)/shard_map/all_gather | solution.py:270
  827.0 6.9 copy-start.28
  827.0 6.9 copy-start.27
  949.1 10.3 %copy-start.18 = (bf16[1024,512]{1,0:T(8,128)(2,1)S(1)}, bf16[1024,512]{1,0:T(8,128)(2,1)}, u32[]{:S(2)}) copy-start(bf16[1024,512]{1,0:T(8,128)(2,1)} %get-tuple-element.139) | copy-start | bytes 3145732
  (12 other events, 36.9 us)
Sparse Core Ops, SparseCore 0:
  22.0 47.3 all-gather.30
  71.5 44.4 all-gather.14
  200.9 29.9 reduce-scatter.12
  337.4 22.5 all-gather.24
  408.1 22.5 all-gather.26
  564.1 43.6 reduce-scatter.20
  610.7 42.8 reduce-scatter.18
  656.4 31.0 reduce-scatter.32
  689.8 31.8 reduce-scatter.34
  723.8 14.6 reduce-scatter.30
  741.3 14.6 reduce-scatter.28
  758.6 14.6 reduce-scatter.26
  776.1 14.6 reduce-scatter.24
  793.8 31.1 reduce-scatter.22
  827.7 121.4 all-reduce.8
Sparse Core Ops, SparseCore 1:
  202.8 31.7 all-gather.18
  236.6 22.4 all-gather.16
  260.5 32.9 all-gather.20
  299.5 31.2 reduce-scatter.14
  371.5 31.2 reduce-scatter.16
  669.3 21.6 all-gather.22
  827.1 22.5 all-gather.28
where the time goes:
time: 978 us; the launch traced here: 973 us
  waiting for transfers between devices  529 us (54%)
  matrix products  246 us (25%)
  blocking collectives  86.4 us (9%)
  other arithmetic  78 us (8%)
  between operations  19.7 us (2%)
  local copies, waits for them, and re-layouts  12 us (1%)
    reduce_scatter x4, waiting for transfers between devices, reduce_heads(): lax.psum_scatter(partial_sum.astype(jnp.bfloat16), 'tp', scatter_dimensio...  109 us
    psum x1, waiting for transfers between devices, body(): lax.psum(shares[0].astype(jnp.bfloat16), 'ctx').astype(jnp.float32)  90.2 us
    all_gather x3, waiting for transfers between devices, spread_rows(): return lax.all_gather(rows_low, 'tp', axis=0, tiled=True)  67.4 us
    dot_general x2, matrix products, masked_scores(): jnp.einsum('sqhd,skhd->shqk', queries, key_piece, preferred_element_type=...  49 us
    all_gather x1, waiting for transfers between devices, body(): key_piece = lax.all_gather(keys, 'ctx', axis=1, tiled=True)  46.2 us
    reduce_scatter x1, waiting for transfers between devices, body(): lax.psum_scatter(key_grad_all.astype(jnp.bfloat16), 'ctx', scatter_dimens...  43.1 us
    dot_general x1, matrix products, backward_update(): jnp.einsum('sqhd,skhd->shqk', heads_grad, backward_value_piece, preferred...  41.9 us
    reduce_scatter x1, waiting for transfers between devices, body(): lax.psum_scatter(down_grad.astype(jnp.bfloat16), 'dp', scatter_dimension=...  34.2 us
  transfers between devices with their start and end apart: 22, of which 18 were waited for; matrix products, arithmetic and copies ran while one was open for 8% of the time, Pallas kernels for 0%

commit v1 on v0

--- a/solution.py
+++ b/solution.py
@@ -314,7 +314,7 @@
         ).astype(jnp.float32),
     )
     totals = (
-        lax.psum(shares[0].astype(jnp.bfloat16), "ctx").astype(jnp.float32),
+        jnp.sum(lax.all_gather(shares[0].astype(jnp.bfloat16), "ctx"), axis=0).astype(jnp.float32),
         lax.psum(shares[1].astype(jnp.bfloat16), "ctx").astype(jnp.float32),
         lax.psum(shares[2].astype(jnp.bfloat16), "ctx").astype(jnp.float32),
         lax.psum(shares[3].astype(jnp.bfloat16), "ctx").astype(jnp.float32),

time: 978 us -> 944 us (0.965)
  waiting for transfers between devices: 529 us -> 494 us
    psum x1, waiting for transfers between devices: 90.2 us -> 40.9 us  [body(): lax.psum(shares[1].astype(jnp.bfloat16), 'ctx').astype(jnp.float32)]
    reduce_scatter x1, waiting for transfers between devices: 20.3 us -> 34.7 us  [body(): lax.psum_scatter(in_grad.astype(jnp.bfloat16), 'dp', scatter_dimension=0,...]
    all_gather x1, waiting for transfers between devices: 0.01 us -> 13.3 us  [body(): lax.all_gather(input_grad.astype(jnp.bfloat16), 'tp', axis=0, tiled=True)]
    reduce_scatter x1, waiting for transfers between devices: 17.5 us -> 5.5 us  [body(): lax.psum_scatter(query_weight_grad.astype(jnp.bfloat16), 'dp', scatter_di...]
  transfers between devices with their start and end apart: 22 -> 23, of which waited for: 18 -> 19; matrix products, arithmetic and copies ran while one was open for 8% -> 9% of each run, Pallas kernels for 0% -> 0%
where the time goes in v1:
time: 944 us; the launch traced here: 939 us
  waiting for transfers between devices  494 us (52%)
  matrix products  245 us (26%)
  blocking collectives  86.2 us (9%)
  other arithmetic  79.8 us (8%)
  between operations  19.8 us (2%)
  local copies, waits for them, and re-layouts  12.1 us (1%)
    reduce_scatter x4, waiting for transfers between devices, reduce_heads(): lax.psum_scatter(partial_sum.astype(jnp.bfloat16), 'tp', scatter_dimensio...  108 us
    all_gather x3, waiting for transfers between devices, spread_rows(): return lax.all_gather(rows_low, 'tp', axis=0, tiled=True)  67.4 us
    dot_general x2, matrix products, masked_scores(): jnp.einsum('sqhd,skhd->shqk', queries, key_piece, preferred_element_type=...  49 us
    all_gather x1, waiting for transfers between devices, body(): key_piece = lax.all_gather(keys, 'ctx', axis=1, tiled=True)  46.1 us
    reduce_scatter x1, waiting for transfers between devices, body(): lax.psum_scatter(key_grad_all.astype(jnp.bfloat16), 'ctx', scatter_dimens...  43 us
    dot_general x1, matrix products, backward_update(): jnp.einsum('sqhd,skhd->shqk', heads_grad, backward_value_piece, preferred...  41.9 us
    psum x1, waiting for transfers between devices, body(): lax.psum(shares[1].astype(jnp.bfloat16), 'ctx').astype(jnp.float32)  40.9 us
    reduce_scatter x1, waiting for transfers between devices, body(): lax.psum_scatter(in_grad.astype(jnp.bfloat16), 'dp', scatter_dimension=0,...  34.7 us
  transfers between devices with their start and end apart: 23, of which 19 were waited for; matrix products, arithmetic and copies ran while one was open for 9% of the time, Pallas kernels for 0%

profile of v1, /device:TPU:0, one launch (start us, length us, event | category | flops | bytes accessed | tf_op | source)
XLA Modules:
  0.0 939.3 jit_solution(18179581941446967045)
XLA Ops:
  8.1 10.4 %all_gather.69 = bf16[1024,256]{1,0:T(8,128)(2,1)S(1)} all-gather(bf16[512,256]{1,0:T(8,128)(2,1)} %param.23), channel_id=1, replica_groups=mesh['dp'=2,'ctx'=4,'tp'=4] {'dp'}, dimensions={0}, use_global_device_ids=true | all-gather | bytes 786432 | tf_op jit(solution)/shard_map/all_gather | solution.py:75
  21.9 8.1 all_gather.67
  30.3 7.3 all_gather.66
  45.1 13.8 %all_gather.65 = s32[1,4096]{1,0:T(1,128)S(1)} all-gather(s32[1,1024]{1,0:T(1,128)S(1)} %copy-done.26), channel_id=1, replica_groups=mesh['dp'=2,'ctx'=4,'tp'=4] {'ctx'}, dimensions={1}, use_global_device_ids=true | all-gather | bytes 20480 | tf_op jit(solution)/shard_map/all_gather | solution.py:86
  62.8 7.0 all_gather.71
  69.8 46.1 %all-gather.17.cloned.1.call-done = bf16[1,4096,4,64]{1,3,2,0:T(8,128)(2,1)} async-done(((bf16[1,1024,4,64]{1,3,2,0:T(8,128)(2,1)}), bf16[1,4096,4,64]{1,3,2,0:T(8,128)(2,1)}) %all-gather.17.cloned.1.call-update) | async-done | bytes 2097168 | tf_op jit(solution)/shard_map/all_gather | solution.py:133
  116.0 81.1 %conditional.2 = (f32[1,4,1024]{2,1,0:T(4,128)S(1)}, f32[1,4,1024]{2,1,0:T(4,128)}, f32[1,1024,4,64]{1,3,2,0:T(8,128)S(1)}, f32[1,4,1024]{2,1,0:T(4,128)S(1)}) conditional(s32[]{:T(128)} %convert_element_type.304, () %tuple.32, (s32[1,1024]{1,0:T(1,128)S(1)}, s32[1,4096]{1,0:T(1,128)S(1)}, bf16[1,1024,4,64]{1,3,2,0:T(8,128)(2,1)S(1)}, ...), branch_computations={%region_4.0_spmd, %region_5.8_spmd} | conditional | flops 4483981312 | bytes 232476736 | solution.py:153
  116.3 4.7 broadcast_compare_fusion
  121.0 25.9 %fusion = (f32[4,1024]{1,0:T(4,128)S(1)}, f32[4,1024,4096]{2,1,0:T(8,128)}) fusion(pred[1024,4096]{1,0:T(8,128)(4,1)} %broadcast_compare_fusion, bf16[1,4096,4,64]{1,3,2,0:T(8,128)(2,1)S(1)} %copy-done.2, bf16[1,1024,4,64]{1,3,2,0:T(8,128)(2,1)S(1)} %get-tuple-element.51), kind=kOutput, calls=%fused_computation.2 | convolution fusion | flops 2197811200 | bytes 73940992 | tf_op jit(solution)/shard_map/cond/branch_1_fun/sqhd,skhd->shqk/dot_general | solution.py:122
  146.9 23.3 %fusion.2 = f32[4,1024]{1,0:T(4,128)} fusion(f32[4,1024,4096]{2,1,0:T(8,128)} %get-tuple-element.154, f32[4,1024]{1,0:T(4,128)S(1)} %broadcast_maximum_fusion, pred[1024,4096]{1,0:T(8,128)(4,1)} %broadcast_compare_fusion), kind=kLoop, calls=%fused_computation.4 | loop fusion | flops 67104768 | bytes 71335936 | tf_op jit(solution)/shard_map/cond/branch_1_fun/reduce_sum | solution.py:143
  171.0 26.1 %fusion.14 = f32[1,1024,4,64]{1,3,2,0:T(8,128)S(1)} fusion(bf16[1,4096,4,64]{1,3,2,0:T(8,128)(2,1)} %get-tuple-element.53, f32[4,1024,4096]{2,1,0:T(8,128)} %get-tuple-element.154, f32[4,1024]{1,0:T(4,128)S(1)} %broadcast_maximum_fusion, pred[1024,4096]{1,0:T(8,128)(4,1)} %broadcast_compare_fusion, f32[1024,4]{0,1:T(4,128)S(1)} %get-tuple-element.143), kind=kOutput, calls=%fused_computation.12 | convolution fusion | flops 2214854656 | bytes 74481664 | tf_op jit(solution)/shard_map/cond/branch_1_fun/shqk,skhd->sqhd/dot_general | solution.py:144
  201.6 4.4 all-gather.2
  206.0 4.4 all-gather.3
  210.4 20.6 %reduce-scatter.13.cloned.1.call-done = bf16[256,1024]{1,0:T(8,128)(2,1)} async-done(((bf16[1024,1024]{1,0:T(8,128)(2,1)}), bf16[256,1024]{1,0:T(8,128)(2,1)}) %reduce-scatter.13.cloned.1.call-update) | async-done | bytes 524304 | tf_op jit(solution)/shard_map/reduce_scatter | solution.py:97
  236.9 22.2 %all-gather.19.cloned.1.call-done = bf16[1024,1024]{1,0:T(8,128)(2,1)} async-done(((bf16[256,1024]{1,0:T(8,128)(2,1)}), bf16[1024,1024]{1,0:T(8,128)(2,1)}) %all-gather.19.cloned.1.call-update) | async-done | bytes 2097168 | tf_op jit(solution)/shard_map/all_gather | solution.py:102
  259.1 14.3 %fusion.50 = (bf16[1024,1024]{1,0:T(8,128)(2,1)}, f32[1024,1024]{1,0:T(8,128)}) fusion(bf16[1024,1024]{1,0:T(8,128)(2,1)} %all-gather.19.cloned.1.call-done, bf16[1024,1024]{1,0:T(8,128)(2,1)} %all-gather.21.cloned.1.call-done), kind=kOutput, calls=%fused_computation.46 | convolution fusion | flops 2215641088 | bytes 10485760 | tf_op jit(solution)/shard_map/dot_general | solution.py:161
  273.4 20.1 %all-gather.23.cloned.1.call-done = bf16[1024,1024]{1,0:T(8,128)(2,1)} async-done(((bf16[1024,512]{1,0:T(8,128)(2,1)}), bf16[1024,1024]{1,0:T(8,128)(2,1)}) %all-gather.23.cloned.1.call-update) | async-done | bytes 2097168 | tf_op jit(solution)/shard_map/all_gather | solution.py:78
  293.5 5.9 convolution_convert_fusion.3
  299.6 4.4 all-gather.4
  304.0 4.4 all-gather.5
  308.3 22.5 %reduce-scatter.15.cloned.1.call-done = bf16[256,1024]{1,0:T(8,128)(2,1)} async-done(((bf16[1024,1024]{1,0:T(8,128)(2,1)}), bf16[256,1024]{1,0:T(8,128)(2,1)}) %reduce-scatter.15.cloned.1.call-update) | async-done | bytes 524304 | tf_op jit(solution)/shard_map/reduce_scatter | solution.py:97
  337.6 22.5 %all-gather.27.cloned.1.call-done = bf16[1024,1024]{1,0:T(8,128)(2,1)} async-done(((bf16[256,1024]{1,0:T(8,128)(2,1)}), bf16[1024,1024]{1,0:T(8,128)(2,1)}) %all-gather.27.cloned.1.call-update) | async-done | bytes 2097168 | tf_op jit(solution)/shard_map/all_gather | solution.py:102
  360.1 6.3 fusion.56
  371.6 31.3 %reduce-scatter.17.cloned.1.call-done = bf16[256,1024]{1,0:T(8,128)(2,1)} async-done(((bf16[1024,1024]{1,0:T(8,128)(2,1)}), bf16[256,1024]{1,0:T(8,128)(2,1)}) %reduce-scatter.17.cloned.1.call-update) | async-done | bytes 524304 | tf_op jit(solution)/shard_map/reduce_scatter | solution.py:97
  408.1 22.7 %all-gather.29.cloned.1.call-done = bf16[1024,1024]{1,0:T(8,128)(2,1)} async-done(((bf16[256,1024]{1,0:T(8,128)(2,1)}), bf16[1024,1024]{1,0:T(8,128)(2,1)}) %all-gather.29.cloned.1.call-update) | async-done | bytes 2097168 | tf_op jit(solution)/shard_map/all_gather | solution.py:102
  434.3 130.0 %conditional.3 = (bf16[1,4096,4,64]{1,3,2,0:T(8,128)(2,1)}, bf16[1,4096,4,64]{1,3,2,0:T(8,128)(2,1)}, f32[1,1024,4,32]{1,3,2,0:T(8,128)}, f32[1,1024,4,32]{1,3,2,0:T(8,128)S(1)}) conditional(s32[]{:T(128)} %convert_element_type.304, () %tuple.34, (s32[1,1024]{1,0:T(1,128)S(1)}, s32[1,4096]{1,0:T(1,128)S(1)}, ...), branch_computations={%region_20.21_spmd, %region_21.22_spmd} | conditional | flops 10911748096 | bytes 349294720 | solution.py:228
  434.4 4.7 broadcast_compare_fusion.1
  439.1 23.1 %fusion.34 = f32[4,1024,4096]{2,1,0:T(8,128)} fusion(bf16[1,4096,4,64]{1,3,2,0:T(8,128)(2,1)S(1)} %get-tuple-element.57, bf16[1,1024,4,64]{1,3,2,0:T(8,128)(2,1)S(1)} %get-tuple-element.56), kind=kOutput, calls=%fused_computation.31 | convolution fusion | flops 2147483648 | bytes 69730304 | tf_op jit(solution)/shard_map/cond/branch_1_fun/sqhd,skhd->shqk/dot_general | solution.py:122
  462.2 28.2 %fusion.28 = bf16[1,4096,4,64]{1,3,2,0:T(8,128)(2,1)} fusion(f32[4,1024,4096]{2,1,0:T(8,128)} %fusion.34, f32[4,1024]{1,0:T(4,128)S(1)} %add_bitcast_fusion, pred[1024,4096]{1,0:T(8,128)(4,1)} %broadcast_compare_fusion.1, bf16[1,1024,4,64]{1,3,2,0:T(8,128)(2,1)S(1)} %get-tuple-element.60), kind=kOutput, calls=%fused_computation.27 | convolution fusion | flops 2214592512 | bytes 73940992 | tf_op jit(solution)/shard_map/cond/branch_1_fun/shqk,sqhd->skhd/dot_general | solution.py:203
  490.4 41.9 %multiply_convert_fusion = bf16[4,1024,4096]{2,1,0:T(8,128)(2,1)} fusion(f32[4,1024,4096]{2,1,0:T(8,128)} %fusion.34, f32[4,1024]{1,0:T(4,128)S(1)} %bitcast.240, f32[4,1024]{1,0:T(4,128)S(1)} %add_bitcast_fusion, pred[1024,4096]{1,0:T(8,128)(4,1)} %broadcast_compare_fusion.1, bf16[1,4096,4,64]{1,3,2,0:T(8,128)(2,1)} %get-tuple-element.61, ...), kind=kOutput, calls=%fused_computation.19 | convolution fusion | flops 2248146944 | bytes 107511808 | tf_op jit(solution)/shard_map/cond/branch_1_fun/sqhd,skhd->shqk/dot_general | solution.py:209
  532.3 15.6 %fusion.39 = f32[1,1024,4,64]{1,3,2,0:T(8,128)S(1)} fusion(bf16[4,1024,4096]{2,1,0:T(8,128)(2,1)} %multiply_convert_fusion, bf16[1,4096,4,64]{1,3,2,0:T(8,128)(2,1)S(1)} %copy-done.4), kind=kOutput, calls=%fused_computation.34 | convolution fusion | flops 2147745792 | bytes 36700160 | tf_op jit(solution)/shard_map/cond/branch_1_fun/shqk,skhd->sqhd/dot_general | solution.py:214
  547.9 15.1 %fusion.27 = bf16[1,4096,4,64]{1,3,2,0:T(8,128)(2,1)} fusion(bf16[4,1024,4096]{2,1,0:T(8,128)(2,1)} %multiply_convert_fusion, bf16[1,1024,4,64]{1,3,2,0:T(8,128)(2,1)S(1)} %get-tuple-element.56), kind=kOutput, calls=%fused_computation.26 | convolution fusion | flops 2149580800 | bytes 36175872 | tf_op jit(solution)/shard_map/cond/branch_1_fun/shqk,sqhd->skhd/dot_general | solution.py:223
  565.1 43.0 %reduce-scatter.19.cloned.1.call-done = bf16[1,1024,4,64]{1,3,2,0:T(8,128)(2,1)} async-done(((bf16[1,4096,4,64]{1,3,2,0:T(8,128)(2,1)}), bf16[1,1024,4,64]{1,3,2,0:T(8,128)(2,1)}) %reduce-scatter.19.cloned.1.call-update) | async-done | bytes 524304 | tf_op jit(solution)/shard_map/reduce_scatter | solution.py:232
  613.0 5.9 convolution_convert_fusion.1
  619.0 6.0 convolution_convert_fusion
  628.3 25.6 %reduce-scatter.21.cloned.1.call-done = bf16[1,1024,4,64]{1,3,2,0:T(8,128)(2,1)} async-done(((bf16[1,4096,4,64]{1,3,2,0:T(8,128)(2,1)}), bf16[1,1024,4,64]{1,3,2,0:T(8,128)(2,1)}) %reduce-scatter.21.cloned.1.call-update) | async-done | bytes 524304 | tf_op jit(solution)/shard_map/reduce_scatter | solution.py:235
  665.0 5.5 reduce-scatter.25.cloned.1.call-done
  670.6 34.7 %reduce-scatter.33.cloned.1.call-done = bf16[512,1024]{1,0:T(8,128)(2,1)} async-done(((bf16[1024,1024]{1,0:T(8,128)(2,1)}), bf16[512,1024]{1,0:T(8,128)(2,1)}) %reduce-scatter.33.cloned.1.call-update) | async-done | bytes 1048592 | tf_op jit(solution)/shard_map/reduce_scatter | solution.py:297
  705.3 34.6 %reduce-scatter.35.cloned.1.call-done = bf16[1024,512]{1,0:T(8,128)(2,1)} async-done(((bf16[1024,1024]{1,0:T(8,128)(2,1)}), bf16[1024,512]{1,0:T(8,128)(2,1)}) %reduce-scatter.35.cloned.1.call-update) | async-done | bytes 1048592 | tf_op jit(solution)/shard_map/reduce_scatter | solution.py:300
  739.9 16.9 %reduce-scatter.31.cloned.1.call-done = bf16[256,512]{1,0:T(8,128)(2,1)} async-done(((bf16[256,1024]{1,0:T(8,128)(2,1)}), bf16[256,512]{1,0:T(8,128)(2,1)}) %reduce-scatter.31.cloned.1.call-update) | async-done | bytes 262160 | tf_op jit(solution)/shard_map/reduce_scatter | solution.py:294
  756.8 17.3 %reduce-scatter.29.cloned.1.call-done = bf16[512,256]{0,1:T(8,128)(2,1)} async-done(((bf16[1024,256]{0,1:T(8,128)(2,1)}), bf16[512,256]{0,1:T(8,128)(2,1)}) %reduce-scatter.29.cloned.1.call-update) | async-done | bytes 262160 | tf_op jit(solution)/shard_map/reduce_scatter | solution.py:291
  774.1 17.5 %reduce-scatter.27.cloned.1.call-done = bf16[512,256]{0,1:T(8,128)(2,1)} async-done(((bf16[1024,256]{0,1:T(8,128)(2,1)}), bf16[512,256]{0,1:T(8,128)(2,1)}) %reduce-scatter.27.cloned.1.call-update) | async-done | bytes 262160 | tf_op jit(solution)/shard_map/reduce_scatter | solution.py:288
  791.7 34.1 %reduce-scatter.23.cloned.1.call-done = bf16[256,1024]{1,0:T(8,128)(2,1)} async-done(((bf16[1024,1024]{1,0:T(8,128)(2,1)}), bf16[256,1024]{1,0:T(8,128)(2,1)}) %reduce-scatter.23.cloned.1.call-update) | async-done | bytes 524304 | tf_op jit(solution)/shard_map/reduce_scatter | solution.py:97
  834.4 5.2 all_gather.85
  839.7 5.0 all-reduce.6
  845.0 11.9 %all-reduce.4 = (bf16[512]{0:T(512)(128)(2,1)S(1)}, bf16[512]{0:T(512)(128)(2,1)S(1)}, bf16[512]{0:T(512)(128)(2,1)S(1)}, bf16[512]{0:T(512)(128)(2,1)S(1)}) all-reduce(bf16[512]{0:T(512)(128)(2,1)S(1)} %dynamic-slice.3, bf16[512]{0:T(512)(128)(2,1)S(1)} %dynamic-slice.5, ...), channel_id=1, replica_groups=mesh['dp'=2,'ctx'=4,'tp'=4] {'ctx'}, use_global_device_ids=true, to_apply=%region_43.44 | all-reduce | flops 2048 | bytes 8192 | tf_op jit(solution)/shard_map/psum | solution.py:323
  863.4 40.9 %all-reduce.9.cloned.1.call-done = (bf16[512,256]{0,1:T(8,128)(2,1)}, bf16[512,256]{0,1:T(8,128)(2,1)}, bf16[256,512]{1,0:T(8,128)(2,1)}, bf16[512,1024]{1,0:T(8,128)(2,1)}, bf16[1024,512]{1,0:T(8,128)(2,1)}) async-done(((bf16[512,256]{0,1:T(8,128)(2,1)}, bf16[512,256]{0,1:T(8,128)(2,1)}, bf16[256,512]{1,0:T(8,128)(2,1)}, bf16[512,1024]{1,0:T(8,128)(2,1)}, bf16[1024,512]{1,0:T(8,128)(2,1)}), ...) | async-done | bytes 2883600 | tf_op jit(solution)/shard_map/psum | solution.py:318
  914.4 13.3 %all-gather.31.cloned.1.call-done = bf16[1024,1024]{1,0:T(8,128)(2,1)} async-done(((bf16[256,1024]{1,0:T(8,128)(2,1)}), bf16[1024,1024]{1,0:T(8,128)(2,1)}) %all-gather.31.cloned.1.call-update) | async-done | bytes 2097168 | tf_op jit(solution)/shard_map/all_gather | solution.py:270
  (213 shorter events, 94.1 us)
Async XLA Ops:
  8.0 13.9 %copy-start.30 = (s32[1,1024]{1,0:T(1,128)S(1)}, s32[1,1024]{1,0:T(1,128)}, u32[]{:S(2)}) copy-start(s32[1,1024]{1,0:T(1,128)} %param.20) | copy-start | bytes 12292
  8.0 13.9 %copy-start.23 = (bf16[512,256]{1,0:T(8,128)(2,1)S(1)}, bf16[512,256]{1,0:T(8,128)(2,1)}, u32[]{:S(2)}) copy-start(bf16[512,256]{1,0:T(8,128)(2,1)} %param.22) | copy-start | bytes 786436
  8.0 61.8 %all-gather.33.cloned.1.call-start = ((), (), s32[]{:S(2)}) async-start(), calls=%async_computation.32 | async-start | bytes 2621440 | tf_op jit(solution)/shard_map/all_gather | solution.py:134
  18.4 11.9 %copy-start.5 = (bf16[1024,256]{1,0:T(8,128)(2,1)}, bf16[1024,256]{1,0:T(8,128)(2,1)S(1)}, u32[]{:S(2)}) copy-start(bf16[1024,256]{1,0:T(8,128)(2,1)S(1)} %all_gather.69) | copy-start | bytes 1572868
  18.4 11.9 %copy-start.24 = (bf16[512,256]{1,0:T(8,128)(2,1)S(1)}, bf16[512,256]{1,0:T(8,128)(2,1)}, u32[]{:S(2)}) copy-start(bf16[512,256]{1,0:T(8,128)(2,1)} %param.21) | copy-start | bytes 786436
  21.9 94.1 %all-gather.17.cloned.1.call-start = ((), (), s32[]{:S(2)}) async-start(), calls=%async_computation.12 | async-start | bytes 2621440 | tf_op jit(solution)/shard_map/all_gather | solution.py:133
  30.1 13.7 %copy-start.7 = (bf16[1024,256]{1,0:T(8,128)(2,1)}, bf16[1024,256]{1,0:T(8,128)(2,1)S(1)}, u32[]{:S(2)}) copy-start(bf16[1024,256]{1,0:T(8,128)(2,1)S(1)} %all_gather.67) | copy-start | bytes 1572868
  37.6 6.2 copy-start.9
  43.8 19.0 %copy-start.25 = (bf16[256,512]{1,0:T(8,128)(2,1)S(1)}, bf16[256,512]{1,0:T(8,128)(2,1)}, u32[]{:S(2)}) copy-start(bf16[256,512]{1,0:T(8,128)(2,1)} %param.24) | copy-start | bytes 786436
  45.0 186.0 %reduce-scatter.13.cloned.1.call-start = ((), (), s32[]{:S(2)}) async-start(), calls=%async_computation.13 | async-start | bytes 2621440 | tf_op jit(solution)/shard_map/reduce_scatter | solution.py:97
  69.8 128.1 %copy-start.15 = (bf16[256,1024]{1,0:T(8,128)(2,1)}, bf16[256,1024]{1,0:T(8,128)(2,1)S(1)}, u32[]{:S(2)}) copy-start(bf16[256,1024]{1,0:T(8,128)(2,1)S(1)} %all_gather.71) | copy-start | bytes 1572868
  197.1 8.9 copy-start.32
  200.9 36.0 %all-gather.21.cloned.1.call-start = ((), (), s32[]{:S(2)}) async-start(), calls=%async_computation.15 | async-start | bytes 3145728 | tf_op jit(solution)/shard_map/all_gather | solution.py:77
  201.5 57.6 %all-gather.19.cloned.1.call-start = ((), (), s32[]{:S(2)}) async-start(), calls=%async_computation.14 | async-start | bytes 2621440 | tf_op jit(solution)/shard_map/all_gather | solution.py:102
  236.2 57.3 %all-gather.23.cloned.1.call-start = ((), (), s32[]{:S(2)}) async-start(), calls=%async_computation.16 | async-start | bytes 3145728 | tf_op jit(solution)/shard_map/all_gather | solution.py:78
  236.8 94.0 %reduce-scatter.15.cloned.1.call-start = ((), (), s32[]{:S(2)}) async-start(), calls=%async_computation.17 | async-start | bytes 2621440 | tf_op jit(solution)/shard_map/reduce_scatter | solution.py:97
  293.5 10.4 %copy-start.34 = (bf16[512]{0:T(512)(128)(2,1)S(1)}, bf16[512]{0:T(512)(128)(2,1)}, u32[]{:S(2)}) copy-start(bf16[512]{0:T(512)(128)(2,1)} %param.30) | copy-start | bytes 3076
  293.5 37.3 %copy-start = (bf16[256,1024]{1,0:T(8,128)(2,1)S(1)}, bf16[256,1024]{1,0:T(8,128)(2,1)}, u32[]{:S(2)}) copy-start(bf16[256,1024]{1,0:T(8,128)(2,1)} %reduce-scatter.13.cloned.1.call-done) | copy-start | bytes 1572868
  299.5 60.6 %all-gather.27.cloned.1.call-start = ((), (), s32[]{:S(2)}) async-start(), calls=%async_computation.19 | async-start | bytes 2621440 | tf_op jit(solution)/shard_map/all_gather | solution.py:102
  337.4 65.5 %reduce-scatter.17.cloned.1.call-start = ((), (), s32[]{:S(2)}) async-start(), calls=%async_computation.20 | async-start | bytes 2621440 | tf_op jit(solution)/shard_map/reduce_scatter | solution.py:97
  360.1 7.7 copy-start.35
  371.5 59.3 %all-gather.29.cloned.1.call-start = ((), (), s32[]{:S(2)}) async-start(), calls=%async_computation.21 | async-start | bytes 2621440 | tf_op jit(solution)/shard_map/all_gather | solution.py:102
  408.1 200.0 %reduce-scatter.19.cloned.1.call-start = ((), (), s32[]{:S(2)}) async-start(), calls=%async_computation.22 | async-start | bytes 2621440 | tf_op jit(solution)/shard_map/reduce_scatter | solution.py:232
  434.3 27.9 %copy-start.21 = (bf16[1,1024,4,64]{1,3,2,0:T(8,128)(2,1)}, bf16[1,1024,4,64]{1,3,2,0:T(8,128)(2,1)S(1)}, u32[]{:S(2)}) copy-start(bf16[1,1024,4,64]{1,3,2,0:T(8,128)(2,1)S(1)} %get-tuple-element.60) | copy-start | bytes 1572868 | tf_op jit(solution)/shard_map/cond
  490.4 41.9 %copy-start.4 = (bf16[1,4096,4,64]{1,3,2,0:T(8,128)(2,1)S(1)}, bf16[1,4096,4,64]{1,3,2,0:T(8,128)(2,1)}, u32[]{:S(2)}) copy-start(bf16[1,4096,4,64]{1,3,2,0:T(8,128)(2,1)} %copy-done.3) | copy-start | bytes 6291460 | tf_op jit(solution)/shard_map/cond
  564.3 45.0 %copy-start.17 = (f32[1024,32]{0,1:T(8,128)S(1)}, f32[1024,32]{0,1:T(8,128)}, u32[]{:S(2)}) copy-start(f32[1024,32]{0,1:T(8,128)} %copy-done.16) | copy-start | bytes 393220
  564.3 45.0 %copy-start.22 = (f32[1024,32]{0,1:T(8,128)S(1)}, f32[1024,32]{0,1:T(8,128)}, u32[]{:S(2)}) copy-start(f32[1024,32]{0,1:T(8,128)} %get-tuple-element.168) | copy-start | bytes 393220
  564.3 47.1 %copy-start.11 = (bf16[1,1024,1024]{2,1,0:T(8,128)(2,1)S(1)}, bf16[1,1024,1024]{2,1,0:T(8,128)(2,1)}, u32[]{:S(2)}) copy-start(bf16[1,1024,1024]{2,1,0:T(8,128)(2,1)} %param.18) | copy-start | bytes 6291460
  564.3 89.5 %reduce-scatter.21.cloned.1.call-start = ((), (), s32[]{:S(2)}) async-start(), calls=%async_computation.23 | async-start | bytes 2621440 | tf_op jit(solution)/shard_map/reduce_scatter | solution.py:235
  565.1 105.4 %reduce-scatter.25.cloned.1.call-start = ((), (), s32[]{:S(2)}) async-start(), calls=%async_computation.26 | async-start | bytes 786432 | tf_op jit(solution)/shard_map/reduce_scatter | solution.py:285
  612.9 92.3 %reduce-scatter.33.cloned.1.call-start = ((), (), s32[]{:S(2)}) async-start(), calls=%async_computation.30 | async-start | bytes 3145728 | tf_op jit(solution)/shard_map/reduce_scatter | solution.py:297
  618.9 120.9 %reduce-scatter.35.cloned.1.call-start = ((), (), s32[]{:S(2)}) async-start(), calls=%async_computation.31 | async-start | bytes 3145728 | tf_op jit(solution)/shard_map/reduce_scatter | solution.py:300
  625.0 32.3 %copy-start.19 = (bf16[1,1024,4,32]{1,3,2,0:T(8,128)(2,1)S(1)}, bf16[1,1024,4,32]{1,3,2,0:T(8,128)(2,1)}, u32[]{:S(2)}) copy-start(bf16[1,1024,4,32]{1,3,2,0:T(8,128)(2,1)} %get-tuple-element.156) | copy-start | bytes 786436
  625.0 131.8 %reduce-scatter.31.cloned.1.call-start = ((), (), s32[]{:S(2)}) async-start(), calls=%async_computation.29 | async-start | bytes 786432 | tf_op jit(solution)/shard_map/reduce_scatter | solution.py:294
  628.2 145.9 %reduce-scatter.29.cloned.1.call-start = ((), (), s32[]{:S(2)}) async-start(), calls=%async_computation.28 | async-start | bytes 786432 | tf_op jit(solution)/shard_map/reduce_scatter | solution.py:291
  653.8 6.7 copy-start.10
  657.2 134.4 %reduce-scatter.27.cloned.1.call-start = ((), (), s32[]{:S(2)}) async-start(), calls=%async_computation.27 | async-start | bytes 786432 | tf_op jit(solution)/shard_map/reduce_scatter | solution.py:288
  660.5 165.3 %reduce-scatter.23.cloned.1.call-start = ((), (), s32[]{:S(2)}) async-start(), calls=%async_computation.24 | async-start | bytes 2621440 | tf_op jit(solution)/shard_map/reduce_scatter | solution.py:97
  664.2 161.6 %copy-start.12 = (f32[256,1024]{1,0:T(8,128)S(1)}, f32[256,1024]{1,0:T(8,128)}, u32[]{:S(2)}) copy-start(f32[256,1024]{1,0:T(8,128)} %get-tuple-element.146) | copy-start | bytes 3145732
  664.2 164.8 %copy-start.36 = (u32[32]{0:T(128)S(1)}, u32[32]{0:T(128)}, u32[]{:S(2)}) copy-start(u32[32]{0:T(128)} %constant.142) | copy-start | bytes 388
  664.2 166.0 %copy-start.27 = (bf16[1024]{0:T(1024)(128)(2,1)S(1)}, bf16[1024]{0:T(1024)(128)(2,1)}, u32[]{:S(2)}) copy-start(bf16[1024]{0:T(1024)(128)(2,1)} %get-tuple-element.117) | copy-start | bytes 6148
  664.2 166.0 %all-gather.25.cloned.1.call-start = ((), (), s32[]{:S(2)}) async-start(), calls=%async_computation.18 | async-start | bytes 2621440 | tf_op jit(solution)/shard_map/all_gather | solution.py:269
  665.0 194.3 %all-gather.35.cloned.1.call-start = ((), (), s32[]{:S(2)}) async-start(), calls=%async_computation.33 | async-start | bytes 1310720 | tf_op jit(solution)/shard_map/all_gather | solution.py:317
  670.5 233.7 %all-reduce.9.cloned.1.call-start = ((), (), s32[]{:S(2)}) async-start(), calls=%async_computation.34 | async-start | bytes 5767168 | tf_op jit(solution)/shard_map/psum | solution.py:318
  791.7 136.0 %all-gather.31.cloned.1.call-start = ((), (), s32[]{:S(2)}) async-start(), calls=%async_computation.25 | async-start | bytes 2621440 | tf_op jit(solution)/shard_map/all_gather | solution.py:270
  827.8 6.6 copy-start.29
  827.8 6.6 copy-start.28
  904.3 8.5 copy-start.18
  (13 other events, 47.5 us)
Sparse Core Ops, SparseCore 0:
  22.0 47.3 all-gather.32
  71.5 44.4 all-gather.16
  201.0 29.9 reduce-scatter.12
  337.5 22.5 all-gather.26
  408.2 22.5 all-gather.28
  564.4 43.6 reduce-scatter.18
  611.0 42.8 reduce-scatter.20
  656.7 13.8 reduce-scatter.24
  673.3 31.8 reduce-scatter.32
  707.9 31.8 reduce-scatter.34
  742.1 14.6 reduce-scatter.30
  759.5 14.6 reduce-scatter.28
  776.9 14.6 reduce-scatter.26
  794.6 31.1 reduce-scatter.22
Sparse Core Ops, SparseCore 1:
  202.9 31.7 all-gather.20
  236.7 22.4 all-gather.18
  260.6 32.9 all-gather.22
  299.6 31.2 reduce-scatter.14
  371.6 31.2 reduce-scatter.16
  667.2 21.6 all-gather.24
  690.2 27.9 all-gather.34
  791.7 112.5 all-reduce.8
  906.3 21.3 all-gather.30
